TPU v7x, 128 devices: a whole 4x4x4 slice. The times are simulated.
128 devices in a mesh: walk: 4 (over y_hi, core), stretch: 32 (over z, y_lo, x).
Axes of the slice: x: 4, y: 4 (y_hi: 2, y_lo: 2; y = y_hi * 2 + y_lo), z: 4, core: 2. Of those that a mesh axis runs over, the one named last changes fastest.
Arguments:
- walkers: float32 [256, 48, 512], P(('walk', 'stretch')), may hold values from -6 to 6
- inverse_intersection: float32 [256, 48, 48], P(('walk', 'stretch')), may hold values from -0.875 to 0.875
- half_rotated: bfloat16 [1024, 48, 512], P('stretch'), may hold values from -0.076546554 to 0.076546554
- cholesky: bfloat16 [1024, 512, 512], P('stretch'), may hold values from -0.015625 to 0.015625
- field_noise: float32 [256, 1024], P('walk', 'stretch'), may hold values from -6 to 6
- branch_sources: int32 [256], P(('walk', 'stretch')), may hold values from 0 to 255, as said below
Outputs:
- force_bias: float32 [256, 1024], P('walk', 'stretch')
- exchange_energy: float32 [256], P(('walk', 'stretch'))
- new_walkers: float32 [256, 48, 512], P(('walk', 'stretch'))
Inputs may be any that keep to these rules, and one draw needn't show every extreme that they name: `branch_sources`: walker d lies in column (d // 2) % 32; every entry names a walker of the same column as its destination slot. A walker may be named by several slots or by none.
All inputs are finite; a program needn't handle non-finite values.
Results may differ from a plain program's by a relative error of at most 0.0029.
Values may be sent and summed in bfloat16 or wider, within the bound.
No kernel may reach another device: no remote copies, remote signals or barrier semaphores. Data moves between devices by JAX's collectives and lax.ppermute only.
A program may use at most 256 MiB of HBM per device.

v0:
```python
import math

import jax
import jax.numpy as jnp
from jax import lax
from jax.sharding import PartitionSpec as P

ORDERS = 2


def apply_rows(psi_rows, field_rows, chol_flat, orbital_count):
    row_count = psi_rows.shape[0]
    occupied = psi_rows.shape[1]
    block_size = math.gcd(row_count, 16)
    blocks = row_count // block_size

    def one_block(operands):
        psi_block, field_block = operands
        matrix = jnp.dot(field_block, chol_flat, preferred_element_type=jnp.float32).reshape(
            block_size, orbital_count, orbital_count
        )
        return jnp.einsum(
            "bip,bpq->biq", psi_block.astype(jnp.float32), matrix, precision=lax.Precision.HIGHEST
        )

    result = lax.map(
        one_block,
        (
            psi_rows.reshape(blocks, block_size, occupied, orbital_count),
            field_rows.reshape(blocks, block_size, field_rows.shape[1]),
        ),
    )
    return result.reshape(row_count, occupied, orbital_count)


def shards(walkers, inverse_intersection, half_rotated, cholesky, field_noise, branch_sources):
    walker_count = walkers.shape[0]
    occupied = walkers.shape[1]
    orbital_count = walkers.shape[2]
    local_vectors = half_rotated.shape[0]
    group_size = walker_count * lax.axis_size("stretch")
    green_rows = jnp.einsum(
        "wij,wjp->wip", inverse_intersection, walkers, precision=lax.Precision.HIGHEST
    ).astype(jnp.bfloat16)
    hr_flat = half_rotated.reshape(local_vectors * occupied, orbital_count)
    initial = (
        jnp.zeros((group_size, local_vectors), jnp.float32),
        jnp.zeros((group_size,), jnp.float32),
    )
    visit_shard_rows = lax.all_gather(green_rows, "stretch", axis=0, tiled=True)
    row_count = visit_shard_rows.shape[0]
    intersections = lax.dot_general(
        hr_flat,
        visit_shard_rows.reshape(row_count * occupied, orbital_count),
        (((1,), (1,)), ((), ())),
        preferred_element_type=jnp.float32,
    )
    intersections = intersections.reshape(local_vectors, occupied, row_count, occupied)
    bias_block = 2.0 * jnp.trace(intersections, axis1=1, axis2=3).T
    energy_block = -0.5 * jnp.sum(
        intersections * jnp.transpose(intersections, (0, 3, 2, 1)), axis=(0, 1, 3)
    )
    force_bias = lax.dynamic_update_slice_in_dim(initial[0], bias_block, jnp.int32(0), 0)
    exchange_energy = lax.psum_scatter(energy_block, "stretch", scatter_dimension=0, tiled=True)
    fields = (0.05 * (field_noise - force_bias)).astype(jnp.bfloat16)
    chol_flat = cholesky.reshape(local_vectors, orbital_count * orbital_count)
    propagated = walkers
    psi_local = walkers.astype(jnp.bfloat16)
    for degree in range(1, ORDERS + 1):
        partial_terms = apply_rows(
            lax.all_gather(psi_local, "stretch", axis=0, tiled=True),
            fields,
            chol_flat,
            orbital_count,
        )
        summed = lax.psum_scatter(partial_terms, "stretch", scatter_dimension=0, tiled=True)
        term_local = summed / degree
        propagated = propagated + term_local
        psi_local = term_local.astype(jnp.bfloat16)
    column = lax.all_gather(propagated, "walk", axis=0, tiled=True)
    position = branch_sources // group_size * walker_count + branch_sources % walker_count
    picked = jnp.take(column, position, axis=0)
    return (force_bias, exchange_energy, picked)


def solution(mesh):
    placed = (
        P(("walk", "stretch"), None, None),
        P(("walk", "stretch"), None, None),
        P("stretch", None, None),
        P("stretch", None, None),
        P("walk", "stretch"),
        P(("walk", "stretch")),
    )
    return jax.shard_map(
        shards,
        mesh=mesh,
        in_specs=placed,
        out_specs=(
            P("walk", "stretch"),
            P(("walk", "stretch")),
            P(("walk", "stretch"), None, None),
        ),
        check_vma=False,
    )
```

profile of v0, /device:TPU:1, one launch (start us, length us, event | category | flops | bytes accessed | tf_op | source)
XLA Modules:
  0.0 1079.8 jit_solution(6514313301649321053)
XLA Ops:
  11.0 18.4 %copy.25 = bf16[4,8,512,512]{3,1,2,0:T(8,128)(2,1)} copy(bf16[4,8,512,512]{3,2,1,0:T(8,128)(2,1)} %bitcast.77) | data formatting | bytes 33554432
  29.4 117.5 %all-gather.4.cloned.1.call-done = bf16[64,48,512]{2,1,0:T(8,128)(2,1)} async-done(((bf16[2,48,512]{2,1,0:T(8,128)(2,1)}), bf16[64,48,512]{2,1,0:T(8,128)(2,1)}) %all-gather.4.cloned.1.call-update) | async-done | bytes 3145744 | tf_op jit(solution)/shard_map/all_gather | solution.py:50
  158.0 18.6 %copy.20 = f32[1536,3072]{1,0:T(8,128)} copy(f32[1536,3072]{0,1:T(8,128)} %convolution_bitcast_fusion) | data formatting | bytes 37748736 | tf_op jit(solution)/shard_map/dot_general | solution.py:52
  176.6 37.7 %reshape.45 = f32[32,48,64,48]{3,2,1,0:T(8,128)} reshape(f32[1536,3072]{1,0:T(8,128)} %copy.20) | data formatting | bytes 37748736 | tf_op jit(solution)/shard_map/reshape | solution.py:58
  214.3 57.2 %copy.21 = f32[32,48,64,48]{1,2,3,0:T(8,128)} copy(f32[32,48,64,48]{3,2,1,0:T(8,128)} %reshape.45) | data formatting | bytes 37748736 | tf_op jit(solution)/shard_map/reshape | solution.py:58
  271.5 32.3 %fusion.26 = (f32[64]{0:T(128)}, f32[32,64]{1,0:T(8,128)S(1)}) fusion(f32[32,48,64,48]{3,2,1,0:T(8,128)} %reshape.45, f32[32,48,64,48]{1,2,3,0:T(8,128)} %copy.21, pred[48,48]{1,0:T(8,128)(4,1)S(1)} %iota_compare_fusion), kind=kLoop, calls=%fused_computation.26 | loop fusion | flops 18872256 | bytes 37759488 | tf_op jit(solution)/shard_map/reduce_sum | solution.py:60
  308.0 111.6 %while.20 = (s32[]{:T(128)}, f32[4,16,48,512]{3,2,1,0:T(8,128)}, bf16[4,16,48,512]{3,2,1,0:T(8,128)(2,1)}, bf16[4,16,32]{2,1,0:T(8,128)(2,1)S(1)}, bf16[32,262144]{1,0:T(8,128)(2,1)}, /*index=5*/s32[]{:T(128)}) while((s32[]{:T(128)}, f32[4,16,48,512]{3,2,1,0:T(8,128)}, bf16[4,16,48,512]{3,2,1,0:T(8,128)(2,1)}, ...), condition=%wide.region_4.5_spmd, body=%wide.region_3.4_spmd.sunk | while | flops 2684354560 | bytes 52696136 | solution.py:26
  321.8 14.0 %bitcast_dynamic-update-slice_fusion.4 = f32[4,16,48,512]{3,2,1,0:T(8,128)} fusion(f32[4,16,48,512]{3,2,1,0:T(8,128)} %get-tuple-element.167, s32[]{:T(128)} %get-tuple-element.166, f32[16,512,512]{2,0,1:T(8,128)} %fusion.46, bf16[4,16,48,512]{3,2,1,0:T(8,128)(2,1)} %get-tuple-element.174), kind=kOutput, calls=%fused_computation.6.clone.1 | convolution fusion | flops 2415919104 | bytes 19137536 | tf_op jit(solution)/shard_map/while/body/eval_jaxpr/bip,bpq->biq/dot_general | solution.py:22
  349.7 14.0 %bitcast_dynamic-update-slice_fusion.4 = f32[4,16,48,512]{3,2,1,0:T(8,128)} fusion(f32[4,16,48,512]{3,2,1,0:T(8,128)} %get-tuple-element.167, s32[]{:T(128)} %get-tuple-element.166, f32[16,512,512]{2,0,1:T(8,128)} %fusion.46, bf16[4,16,48,512]{3,2,1,0:T(8,128)(2,1)} %get-tuple-element.174), kind=kOutput, calls=%fused_computation.6.clone.1 | convolution fusion | flops 2415919104 | bytes 19137536 | tf_op jit(solution)/shard_map/while/body/eval_jaxpr/bip,bpq->biq/dot_general | solution.py:22
  363.7 13.8 %fusion.46 = f32[16,512,512]{2,0,1:T(8,128)} fusion(bf16[4,512,8,512]{3,2,1,0:T(8,128)(2,1)} %bitcast.73, bf16[4,16,32]{2,1,0:T(8,128)(2,1)S(1)} %get-tuple-element.175, s32[]{:T(128)} %get-tuple-element.166), kind=kOutput, calls=%fused_computation.1.clone.1 | convolution fusion | flops 268435456 | bytes 33558532 | tf_op jit(solution)/shard_map/while/body/eval_jaxpr/dot_general | solution.py:19
  377.6 14.0 %bitcast_dynamic-update-slice_fusion.4 = f32[4,16,48,512]{3,2,1,0:T(8,128)} fusion(f32[4,16,48,512]{3,2,1,0:T(8,128)} %get-tuple-element.167, s32[]{:T(128)} %get-tuple-element.166, f32[16,512,512]{2,0,1:T(8,128)} %fusion.46, bf16[4,16,48,512]{3,2,1,0:T(8,128)(2,1)} %get-tuple-element.174), kind=kOutput, calls=%fused_computation.6.clone.1 | convolution fusion | flops 2415919104 | bytes 19137536 | tf_op jit(solution)/shard_map/while/body/eval_jaxpr/bip,bpq->biq/dot_general | solution.py:22
  391.6 13.8 %fusion.46 = f32[16,512,512]{2,0,1:T(8,128)} fusion(bf16[4,512,8,512]{3,2,1,0:T(8,128)(2,1)} %bitcast.73, bf16[4,16,32]{2,1,0:T(8,128)(2,1)S(1)} %get-tuple-element.175, s32[]{:T(128)} %get-tuple-element.166), kind=kOutput, calls=%fused_computation.1.clone.1 | convolution fusion | flops 268435456 | bytes 33558532 | tf_op jit(solution)/shard_map/while/body/eval_jaxpr/dot_general | solution.py:19
  405.4 14.1 %bitcast_dynamic-update-slice_fusion.4 = f32[4,16,48,512]{3,2,1,0:T(8,128)} fusion(f32[4,16,48,512]{3,2,1,0:T(8,128)} %get-tuple-element.167, s32[]{:T(128)} %get-tuple-element.166, f32[16,512,512]{2,0,1:T(8,128)} %fusion.46, bf16[4,16,48,512]{3,2,1,0:T(8,128)(2,1)} %get-tuple-element.174), kind=kOutput, calls=%fused_computation.6.clone.1 | convolution fusion | flops 2415919104 | bytes 19137536 | tf_op jit(solution)/shard_map/while/body/eval_jaxpr/bip,bpq->biq/dot_general | solution.py:22
  419.6 175.7 %reduce-scatter.3.cloned.1.call-done = f32[2,48,512]{2,1,0:T(8,128)} async-done(((f32[64,48,512]{2,1,0:T(8,128)}), f32[2,48,512]{2,1,0:T(8,128)}) %reduce-scatter.3.cloned.1.call-update) | async-done | bytes 196624 | tf_op jit(solution)/shard_map/reduce_scatter | solution.py:76
  597.0 151.0 %all-gather.8.cloned.1.call-done = bf16[64,48,512]{2,1,0:T(8,128)(2,1)} async-done(((bf16[2,48,512]{2,1,0:T(8,128)(2,1)}), bf16[64,48,512]{2,1,0:T(8,128)(2,1)}) %all-gather.8.cloned.1.call-update) | async-done | bytes 3145744 | tf_op jit(solution)/shard_map/all_gather | solution.py:71
  751.5 111.7 %while.21 = (s32[]{:T(128)}, f32[4,16,48,512]{3,2,1,0:T(8,128)}, bf16[4,16,48,512]{3,2,1,0:T(8,128)(2,1)}, bf16[4,16,32]{2,1,0:T(8,128)(2,1)S(1)}, bf16[32,262144]{1,0:T(8,128)(2,1)}, /*index=5*/s32[]{:T(128)}) while((s32[]{:T(128)}, f32[4,16,48,512]{3,2,1,0:T(8,128)}, bf16[4,16,48,512]{3,2,1,0:T(8,128)(2,1)}, ...), condition=%wide.region_7.8_spmd, body=%wide.region_6.7_spmd.sunk | while | flops 2684354560 | bytes 52696136 | solution.py:26
  751.5 13.9 %fusion.51 = f32[16,512,512]{2,0,1:T(8,128)} fusion(bf16[4,512,8,512]{3,2,1,0:T(8,128)(2,1)} %bitcast.74, bf16[4,16,32]{2,1,0:T(8,128)(2,1)S(1)} %get-tuple-element.193, s32[]{:T(128)} %get-tuple-element.184), kind=kOutput, calls=%fused_computation.13.clone.1 | convolution fusion | flops 268435456 | bytes 33558532 | tf_op jit(solution)/shard_map/while/body/eval_jaxpr/dot_general | solution.py:19
  765.4 14.0 %bitcast_dynamic-update-slice_fusion.5 = f32[4,16,48,512]{3,2,1,0:T(8,128)} fusion(f32[4,16,48,512]{3,2,1,0:T(8,128)} %get-tuple-element.185, s32[]{:T(128)} %get-tuple-element.184, f32[16,512,512]{2,0,1:T(8,128)} %fusion.51, bf16[4,16,48,512]{3,2,1,0:T(8,128)(2,1)} %get-tuple-element.192), kind=kOutput, calls=%fused_computation.18.clone.1 | convolution fusion | flops 2415919104 | bytes 19137536 | tf_op jit(solution)/shard_map/while/body/eval_jaxpr/bip,bpq->biq/dot_general | solution.py:22
  793.3 14.0 %bitcast_dynamic-update-slice_fusion.5 = f32[4,16,48,512]{3,2,1,0:T(8,128)} fusion(f32[4,16,48,512]{3,2,1,0:T(8,128)} %get-tuple-element.185, s32[]{:T(128)} %get-tuple-element.184, f32[16,512,512]{2,0,1:T(8,128)} %fusion.51, bf16[4,16,48,512]{3,2,1,0:T(8,128)(2,1)} %get-tuple-element.192), kind=kOutput, calls=%fused_computation.18.clone.1 | convolution fusion | flops 2415919104 | bytes 19137536 | tf_op jit(solution)/shard_map/while/body/eval_jaxpr/bip,bpq->biq/dot_general | solution.py:22
  821.2 14.0 %bitcast_dynamic-update-slice_fusion.5 = f32[4,16,48,512]{3,2,1,0:T(8,128)} fusion(f32[4,16,48,512]{3,2,1,0:T(8,128)} %get-tuple-element.185, s32[]{:T(128)} %get-tuple-element.184, f32[16,512,512]{2,0,1:T(8,128)} %fusion.51, bf16[4,16,48,512]{3,2,1,0:T(8,128)(2,1)} %get-tuple-element.192), kind=kOutput, calls=%fused_computation.18.clone.1 | convolution fusion | flops 2415919104 | bytes 19137536 | tf_op jit(solution)/shard_map/while/body/eval_jaxpr/bip,bpq->biq/dot_general | solution.py:22
  849.1 14.1 %bitcast_dynamic-update-slice_fusion.5 = f32[4,16,48,512]{3,2,1,0:T(8,128)} fusion(f32[4,16,48,512]{3,2,1,0:T(8,128)} %get-tuple-element.185, s32[]{:T(128)} %get-tuple-element.184, f32[16,512,512]{2,0,1:T(8,128)} %fusion.51, bf16[4,16,48,512]{3,2,1,0:T(8,128)(2,1)} %get-tuple-element.192), kind=kOutput, calls=%fused_computation.18.clone.1 | convolution fusion | flops 2415919104 | bytes 19137536 | tf_op jit(solution)/shard_map/while/body/eval_jaxpr/bip,bpq->biq/dot_general | solution.py:22
  864.5 69.6 %all-reduce = f32[64]{0:T(128)S(1)} all-reduce(f32[64]{0:T(128)S(1)} %broadcast_multiply_fusion), channel_id=2, replica_groups=mesh['walk'=4,'stretch'=32] {'stretch'}, use_global_device_ids=true, to_apply=%region_2.3.clone | all-reduce | flops 64 | bytes 512
  934.7 104.5 %reduce-scatter.5.cloned.1.call-done = f32[2,48,512]{2,1,0:T(8,128)} async-done(((f32[64,48,512]{2,1,0:T(8,128)}), f32[2,48,512]{2,1,0:T(8,128)}) %reduce-scatter.5.cloned.1.call-update) | async-done | bytes 196624 | tf_op jit(solution)/shard_map/reduce_scatter | solution.py:76
  1040.1 31.9 %all_gather.15 = f32[8,48,512]{2,1,0:T(8,128)S(1)} all-gather(f32[2,48,512]{2,1,0:T(8,128)S(1)} %multiply_add_fusion), channel_id=1, replica_groups=mesh['walk'=4,'stretch'=32] {'walk'}, dimensions={0}, use_global_device_ids=true | all-gather | bytes 983040 | tf_op jit(solution)/shard_map/all_gather | solution.py:80
  (49 shorter events, 96.8 us)
Async XLA Ops:
  7.2 139.8 %copy-start = (bf16[32,48,512]{2,1,0:T(8,128)(2,1)S(1)}, bf16[32,48,512]{2,1,0:T(8,128)(2,1)}, u32[]{:S(2)}) copy-start(bf16[32,48,512]{2,1,0:T(8,128)(2,1)} %param.12) | copy-start | bytes 4718596
  7.2 139.7 %all-gather.4.cloned.1.call-start = ((), (), s32[]{:S(2)}) async-start(), calls=%async_computation.2 | async-start | bytes 3244032 | tf_op jit(solution)/shard_map/all_gather | solution.py:50
  9.3 295.3 %all-gather.6.cloned.1.call-start = ((), (), s32[]{:S(2)}) async-start(), calls=%async_computation.3 | async-start | bytes 3244032 | tf_op jit(solution)/shard_map/all_gather | solution.py:71
  10.9 584.4 %reduce-scatter.3.cloned.1.call-start = ((), (), s32[]{:S(2)}) async-start(), calls=%async_computation.4 | async-start | bytes 6488064 | tf_op jit(solution)/shard_map/reduce_scatter | solution.py:76
  271.5 32.3 %copy-start.4 = (f32[64,32]{0,1:T(8,128)S(1)}, f32[64,32]{0,1:T(8,128)}, u32[]{:S(2)}) copy-start(f32[64,32]{0,1:T(8,128)} %param.14) | copy-start | bytes 24580
  419.6 328.4 %all-gather.8.cloned.1.call-start = ((), (), s32[]{:S(2)}) async-start(), calls=%async_computation.5 | async-start | bytes 3244032 | tf_op jit(solution)/shard_map/all_gather | solution.py:71
  596.9 442.2 %reduce-scatter.5.cloned.1.call-start = ((), (), s32[]{:S(2)}) async-start(), calls=%async_computation.6 | async-start | bytes 6488064 | tf_op jit(solution)/shard_map/reduce_scatter | solution.py:76
  751.5 111.7 %copy-start.7 = (u32[128]{0:T(128)S(1)}, u32[128]{0:T(128)}, u32[]{:S(2)}) copy-start(u32[128]{0:T(128)} %constant.87) | copy-start | bytes 1540
  751.5 113.0 %copy-start.6 = (s32[2]{0:T(128)S(1)}, s32[2]{0:T(128)}, u32[]{:S(2)}) copy-start(s32[2]{0:T(128)} %param.15) | copy-start | bytes 28
  751.5 113.0 %copy-start.5 = (f32[64]{0:T(128)S(1)}, f32[64]{0:T(128)}, u32[]{:S(2)}) copy-start(f32[64]{0:T(128)} %get-tuple-element.72) | copy-start | bytes 772
  751.5 287.7 %copy-start.2 = (f32[2,48,512]{2,1,0:T(8,128)S(1)}, f32[2,48,512]{2,1,0:T(8,128)}, u32[]{:S(2)}) copy-start(f32[2,48,512]{2,1,0:T(8,128)} %param.10) | copy-start | bytes 589828
  751.5 287.7 %copy-start.3 = (f32[2,48,512]{2,1,0:T(8,128)S(1)}, f32[2,48,512]{2,1,0:T(8,128)}, u32[]{:S(2)}) copy-start(f32[2,48,512]{2,1,0:T(8,128)} %reduce-scatter.3.cloned.1.call-done) | copy-start | bytes 589828
  863.1 210.2 %copy-start.1 = (bf16[32,48,512]{2,1,0:T(8,128)(2,1)S(1)}, bf16[32,48,512]{2,1,0:T(8,128)(2,1)}, u32[]{:S(2)}) copy-start(bf16[32,48,512]{2,1,0:T(8,128)(2,1)} %param.12) | copy-start | bytes 4718596
Sparse Core Ops, SparseCore 0:
  10.2 136.6 all-gather.3
  148.6 154.3 all-gather.5
  419.7 175.6 reduce-scatter.2
  597.4 150.5 all-gather.7
  863.3 175.7 reduce-scatter.4
where the time goes:
time: 1080 us
  waiting for transfers between devices  549 us (51%)
  matrix products  236 us (22%)
  local copies, waits for them, and re-layouts  141 us (13%)
  blocking collectives  101 us (9%)
  other arithmetic  37.9 us (4%)
  between operations  14.5 us (1%)
    reduce_scatter x2, waiting for transfers between devices, shards(): lax.psum_scatter(partial_terms, 'stretch', scatter_dimension=0, tiled=True)  280 us
    all_gather x2, waiting for transfers between devices, shards(): lax.all_gather(psi_local, 'stretch', axis=0, tiled=True)  151 us
    all_gather x1, waiting for transfers between devices, shards(): visit_shard_rows = lax.all_gather(green_rows, 'stretch', axis=0, tiled=True)  118 us
    dot_general x8, matrix products, one_block(): jnp.einsum('bip,bpq->biq', psi_block.astype(jnp.float32), matrix, precisi...  112 us
    dot_general x8, matrix products, one_block(): jnp.dot(field_block, chol_flat, preferred_element_type=jnp.float32)  111 us
    reshape x2, local copies, waits for them, and re-layouts, shards(): intersections.reshape(local_vectors, occupied, row_count, occupied)  94.9 us
    unnamed x1, blocking collectives  69.6 us
    reduce_sum x1, other arithmetic, shards(): jnp.sum(intersections * jnp.transpose(intersections, (0, 3, 2, 1)), axis=...  32.3 us
  transfers between devices with their start and end apart: 5, of which 4 were waited for; matrix products, arithmetic and copies ran while one was open for 17% of the time, Pallas kernels for 0%

commit v1 on v0

v1 whole, which is shorter than its diff:
```python
import functools

import jax
import jax.numpy as jnp
import numpy as np
from jax import lax
from jax.experimental import pallas as pl
from jax.experimental.pallas import tpu as pltpu
from jax.sharding import PartitionSpec as P

ORDERS = 2
Z, Y, X = 4, 2, 4
S = Z * Y * X
STEP = {"z": (1, 0, 0), "y": (0, 1, 0), "x": (0, 0, 1)}
HEARD = (0, -1, 1, -2)
ORDER_A = "yxz"
ORDER_B = "yzx"
PAD = 64
WB = 8
F32 = jnp.float32
BF16 = jnp.bfloat16


def encode(z, y, x):
    return (z % Z) * (Y * X) + (y % Y) * X + (x % X)


def decode(s):
    return s // (Y * X), s // X % Y, s % X


def shift(a, axis, k):
    d = STEP[axis]
    pairs = []
    for s in range(S):
        z, y, x = decode(s)
        pairs.append((s, encode(z + d[0] * k, y + d[1] * k, x + d[2] * k)))
    return lax.ppermute(a, "stretch", pairs)


def gather_staged(a, order):
    for axis in order:
        if axis == "y":
            a = jnp.concatenate([a, shift(a, axis, 1)], 0)
        else:
            a = jnp.concatenate([a, shift(a, axis, 1), shift(a, axis, -1), shift(a, axis, 2)], 0)
    return a


def slots(order):
    table = np.zeros((S, S), np.int32)
    for s in range(S):
        offsets = [(0, 0, 0)]
        for axis in order:
            d = STEP[axis]
            heard = HEARD[:2] if axis == "y" else HEARD
            offsets = [tuple(o[i] + d[i] * h for i in range(3)) for h in heard for o in offsets]
        z, y, x = decode(s)
        for slot, o in enumerate(offsets):
            table[s, encode(z + o[0], y + o[1], x + o[2])] = slot
    return table


def gather_walkers(a):
    return gather_staged(a[0:1], ORDER_A), gather_staged(a[1:2], ORDER_B)


def intersect_kernel(slot_ref, ga_ref, gb_ref, he_ref, ho_ref, ht_ref, hts_ref, e_ref, s_ref, gp, gps, ge, go):
    @pl.when(pl.program_id(0) == 0)
    def _():
        gp[...] = jnp.zeros_like(gp)
        gps[...] = jnp.zeros_like(gps)

    nocc = ga_ref.shape[1]
    base = pl.program_id(0) * (WB // 2)
    for k in range(WB // 2):
        a = ga_ref[slot_ref[0, base + k]]
        b = gb_ref[slot_ref[1, base + k]]
        gp[2 * k * PAD : 2 * k * PAD + nocc, :] = a
        gp[(2 * k + 1) * PAD : (2 * k + 1) * PAD + nocc, :] = b
        gps[(2 * k + 1) * PAD : (2 * k + 1) * PAD + nocc, :] = a
        gps[2 * k * PAD : 2 * k * PAD + nocc, :] = b
        ge[k * nocc : (k + 1) * nocc, :] = a
        go[k * nocc : (k + 1) * nocc, :] = b
    nt = (((1,), (1,)), ((), ()))
    ae = lax.dot_general(he_ref[...], gp[...], nt, preferred_element_type=F32)
    ao = lax.dot_general(ho_ref[...], gps[...], nt, preferred_element_type=F32)
    be = jnp.dot(ge[...], ht_ref[...], preferred_element_type=F32)
    bo = jnp.dot(go[...], hts_ref[...], preferred_element_type=F32)
    lane = lax.broadcasted_iota(jnp.int32, (8, 128), 1)
    row = lax.broadcasted_iota(jnp.int32, (8, 128), 0)
    low = lane < PAD
    group = lane % PAD // 8
    diagonal = (lane % 8 == row) & (lane % PAD < nocc)
    tiles = nocc // 8
    g_pairs = he_ref.shape[0] // nocc
    for k in range(WB // 2):
        acc_e = jnp.zeros((8, 128), F32)
        acc_o = jnp.zeros((8, 128), F32)
        for g in range(g_pairs):
            de = do = None
            for t in range(tiles):
                rg = slice(g * nocc + t * 8, g * nocc + t * 8 + 8)
                rw = slice(k * nocc + t * 8, k * nocc + t * 8 + 8)
                lw = slice(k * 128, k * 128 + 128)
                lg = slice(g * 128, g * 128 + 128)
                a0, a1 = ae[rg, lw], ao[rg, lw]
                c0, c1 = be[rw, lg], bo[rw, lg]
                acc_e += a0 * jnp.where(low, c0, c1)
                acc_o += a1 * jnp.where(low, c1, c0)
                de = a0 if t == 0 else jnp.where(group == t, a0, de)
                do = a1 if t == 0 else jnp.where(group == t, a1, do)
            s_ref[k, 0, g : g + 1, :] = jnp.sum(jnp.where(diagonal, de, 0.0), axis=0, keepdims=True)
            s_ref[k, 1, g : g + 1, :] = jnp.sum(jnp.where(diagonal, do, 0.0), axis=0, keepdims=True)
        e_ref[k, 0] = acc_e
        e_ref[k, 1] = acc_o


def intersect(table, ga, gb, half_rotated):
    vectors, nocc, m = half_rotated.shape
    walkers = 2 * ga.shape[0]
    he = half_rotated[0::2].reshape(vectors // 2 * nocc, m)
    ho = half_rotated[1::2].reshape(vectors // 2 * nocc, m)
    padded = jnp.pad(half_rotated, ((0, 0), (0, PAD - nocc), (0, 0)))
    swapped = padded.reshape(vectors // 2, 2, PAD, m)[:, ::-1]
    ht = padded.reshape(vectors * PAD, m).T
    hts = swapped.reshape(vectors * PAD, m).T
    steps = walkers // WB
    vmem = pl.BlockSpec(memory_space=pltpu.VMEM)
    sums, diag = pl.pallas_call(
        intersect_kernel,
        grid=(steps,),
        in_specs=[pl.BlockSpec(memory_space=pltpu.SMEM)] + [vmem] * 6,
        out_specs=[
            pl.BlockSpec((WB // 2, 2, 8, 128), lambda i: (i, 0, 0, 0)),
            pl.BlockSpec((WB // 2, 2, vectors // 2, 128), lambda i: (i, 0, 0, 0)),
        ],
        out_shape=[
            jax.ShapeDtypeStruct((walkers // 2, 2, 8, 128), F32),
            jax.ShapeDtypeStruct((walkers // 2, 2, vectors // 2, 128), F32),
        ],
        scratch_shapes=[
            pltpu.VMEM((WB * PAD, m), BF16),
            pltpu.VMEM((WB * PAD, m), BF16),
            pltpu.VMEM((WB // 2 * nocc, m), BF16),
            pltpu.VMEM((WB // 2 * nocc, m), BF16),
        ],
        compiler_params=pltpu.CompilerParams(vmem_limit_bytes=60 << 20),
        cost_estimate=pl.CostEstimate(
            flops=4 * vectors * nocc * walkers * PAD * m, bytes_accessed=16 << 20, transcendentals=0
        ),
        name="intersect",
    )(table, ga, gb, he, ho, ht, hts)
    halves = jnp.sum(diag.reshape(walkers // 2, 2, vectors // 2, 2, PAD), -1)
    even, odd = halves[:, 0], halves[:, 1, :, ::-1]
    bias = 2.0 * jnp.stack([even, odd], 2)
    bias = jnp.transpose(bias, (0, 3, 1, 2)).reshape(walkers, vectors)
    parts = jnp.sum(sums.reshape(walkers // 2, 2, 8, 2, PAD), (2, 4))
    energy = -0.5 * (parts[:, 0] + parts[:, 1, ::-1]).reshape(walkers)
    return bias, energy


def field_kernel(slot_ref, f_ref, pa_ref, pb_ref, c_ref, h_ref, o_ref, fbd, hold):
    step = pl.program_id(0)
    walkers, vectors = f_ref.shape
    m = c_ref.shape[2]

    @pl.when(step == 0)
    def _():
        rows, cols = walkers * 8, vectors * 8
        r = lax.broadcasted_iota(jnp.int32, (rows, walkers), 0) // 8
        w = lax.broadcasted_iota(jnp.int32, (rows, walkers), 1)
        pick_w = jnp.where(r == w, 1.0, 0.0).astype(BF16)
        v = lax.broadcasted_iota(jnp.int32, (vectors, cols), 0)
        c = lax.broadcasted_iota(jnp.int32, (vectors, cols), 1) // 8
        pick_v = jnp.where(v == c, 1.0, 0.0).astype(BF16)
        spread = jnp.dot(pick_w, f_ref[...], preferred_element_type=F32).astype(BF16)
        spread = jnp.dot(spread, pick_v, preferred_element_type=F32)
        rr = lax.broadcasted_iota(jnp.int32, (rows, cols), 0) % 8
        cc = lax.broadcasted_iota(jnp.int32, (rows, cols), 1) % 8
        fbd[...] = jnp.where(rr == cc, spread, 0.0).astype(BF16)

    block = c_ref[...].astype(F32)
    lo = block[:, :8, :].reshape(vectors * 8, m).astype(BF16)
    hi = block[:, 8:, :].reshape(vectors * 8, m).astype(BF16)
    hlo = jnp.dot(fbd[...], lo, preferred_element_type=F32).reshape(walkers, 8, m)
    hhi = jnp.dot(fbd[...], hi, preferred_element_type=F32).reshape(walkers, 8, m)
    h = jnp.concatenate([hlo, hhi], axis=1).astype(BF16)
    h_ref[...] = h
    hold[:, pl.ds(pl.multiple_of(step * 16, 16), 16), :] = h

    @pl.when(step == pl.num_programs(0) - 1)
    def _():
        def one(i, carry):
            a = pa_ref[slot_ref[0, i]]
            b = pb_ref[slot_ref[1, i]]
            o_ref[2 * i] = jnp.dot(a, hold[2 * i], preferred_element_type=F32).astype(BF16)
            o_ref[2 * i + 1] = jnp.dot(b, hold[2 * i + 1], preferred_element_type=F32).astype(BF16)
            return carry

        lax.fori_loop(0, walkers // 2, one, 0)


def field_apply(table, fields, pa, pb, cholesky):
    walkers, vectors = fields.shape
    m = cholesky.shape[1]
    nocc = pa.shape[1]
    vmem = pl.BlockSpec(memory_space=pltpu.VMEM)
    return pl.pallas_call(
        field_kernel,
        grid=(m // 16,),
        in_specs=[
            pl.BlockSpec(memory_space=pltpu.SMEM),
            vmem,
            vmem,
            vmem,
            pl.BlockSpec((vectors, 16, m), lambda i: (0, i, 0)),
        ],
        out_specs=[pl.BlockSpec((walkers, 16, m), lambda i: (0, i, 0)), vmem],
        out_shape=[
            jax.ShapeDtypeStruct((walkers, m, m), BF16),
            jax.ShapeDtypeStruct((walkers, nocc, m), BF16),
        ],
        scratch_shapes=[pltpu.VMEM((walkers * 8, vectors * 8), BF16), pltpu.VMEM((walkers, m, m), BF16)],
        compiler_params=pltpu.CompilerParams(vmem_limit_bytes=60 << 20),
        cost_estimate=pl.CostEstimate(flops=12 << 30, bytes_accessed=64 << 20, transcendentals=0),
        name="field_apply",
    )(table, fields, pa, pb, cholesky)


def apply_kernel(slot_ref, pa_ref, pb_ref, h_ref, o_ref):
    pairs = h_ref.shape[0] // 2
    base = pl.program_id(0) * pairs
    for k in range(pairs):
        a = pa_ref[slot_ref[0, base + k]]
        b = pb_ref[slot_ref[1, base + k]]
        o_ref[2 * k] = jnp.dot(a, h_ref[2 * k], preferred_element_type=F32).astype(BF16)
        o_ref[2 * k + 1] = jnp.dot(b, h_ref[2 * k + 1], preferred_element_type=F32).astype(BF16)


def apply(table, pa, pb, h):
    walkers, m, _ = h.shape
    nocc = pa.shape[1]
    vmem = pl.BlockSpec(memory_space=pltpu.VMEM)
    block = 4
    return pl.pallas_call(
        apply_kernel,
        grid=(walkers // block,),
        in_specs=[
            pl.BlockSpec(memory_space=pltpu.SMEM),
            vmem,
            vmem,
            pl.BlockSpec((block, m, m), lambda i: (i, 0, 0)),
        ],
        out_specs=pl.BlockSpec((block, nocc, m), lambda i: (i, 0, 0)),
        out_shape=jax.ShapeDtypeStruct((walkers, nocc, m), BF16),
        compiler_params=pltpu.CompilerParams(vmem_limit_bytes=60 << 20),
        cost_estimate=pl.CostEstimate(flops=6 << 30, bytes_accessed=40 << 20, transcendentals=0),
        name="apply",
    )(table, pa, pb, h)


def scatter_sum(part):
    walkers, nocc, m = part.shape
    got = lax.all_to_all(part.reshape(S, walkers // S, nocc, m), "stretch", 0, 0, tiled=True)
    return jnp.sum(got.astype(F32), 0)


def shards(walkers, inverse_intersection, half_rotated, cholesky, field_noise, branch_sources):
    walker_count = walkers.shape[0]
    group_size = walker_count * S
    place = lax.axis_index("stretch")
    both = np.stack([slots(ORDER_A), slots(ORDER_B)], 1)
    table = lax.dynamic_index_in_dim(jnp.asarray(both), place, 0, keepdims=False)
    green = jnp.einsum(
        "wij,wjp->wip", inverse_intersection, walkers, precision=lax.Precision.HIGHEST
    ).astype(BF16)
    ga, gb = gather_walkers(green)
    pa, pb = gather_walkers(walkers.astype(BF16))
    force_bias, energy = intersect(table, ga, gb, half_rotated)
    fields = (0.05 * (field_noise - force_bias)).astype(BF16)
    h, part = field_apply(table, fields, pa, pb, cholesky)
    got = lax.all_to_all(energy.reshape(S, walker_count), "stretch", 0, 0, tiled=True)
    exchange_energy = jnp.sum(got, 0)
    first = scatter_sum(part)
    qa, qb = gather_walkers(first.astype(BF16))
    second = scatter_sum(apply(table, qa, qb, h)) / 2
    propagated = walkers + first + second
    column = lax.all_gather(propagated, "walk", axis=0, tiled=True)
    position = branch_sources // group_size * walker_count + branch_sources % walker_count
    picked = jnp.take(column, position, axis=0)
    return (force_bias, exchange_energy, picked)


def solution(mesh):
    placed = (
        P(("walk", "stretch"), None, None),
        P(("walk", "stretch"), None, None),
        P("stretch", None, None),
        P("stretch", None, None),
        P("walk", "stretch"),
        P(("walk", "stretch")),
    )
    return jax.shard_map(
        shards,
        mesh=mesh,
        in_specs=placed,
        out_specs=(
            P("walk", "stretch"),
            P(("walk", "stretch")),
            P(("walk", "stretch"), None, None),
        ),
        check_vma=False,
    )
```

time: 1080 us -> 319 us (0.30)
  waiting for transfers between devices: 549 us -> 76.7 us
  matrix products: 236 us -> 1.23 us
  local copies, waits for them, and re-layouts: 141 us -> 49.5 us
  Pallas kernels: 0 us -> 84.5 us
  blocking collectives: 101 us -> 24.2 us
  starting transfers between devices: 0.21 us -> 74.4 us
  other arithmetic: 37.9 us -> 5.4 us
  between operations: 14.5 us -> 1.09 us
    reduce_scatter x2 -> x0, waiting for transfers between devices: 280 us -> none  [shards(): lax.psum_scatter(partial_terms, 'stretch', scatter_dimension=0, tiled=True)]
    all_gather x3 -> x0, waiting for transfers between devices: 269 us -> none  [the longest x2 151 us: shards(): lax.all_gather(psi_local, 'stretch', axis=0, tiled=True)]
    dot_general x17 -> x0, matrix products: 234 us -> none  [the longest x8 112 us: one_block(): jnp.einsum('bip,bpq->biq', psi_block.astype(jnp.float32), matrix, precisi...]
    reshape x2 -> x4, local copies, waits for them, and re-layouts: 94.9 us -> 8.47 us  [the longest x1 4.08 us: intersect(): hts = swapped.reshape(vectors * PAD, m).T]
    pallas_call x0 -> x3, Pallas kernels: none -> 84.5 us  [the longest x1 43.7 us: field_apply(): pl.pallas_call(field_kernel, grid=(m // 16,), in_specs=[pl.BlockSpec(memo...]
    unnamed x1 -> x0, blocking collectives: 69.6 us -> none
    all_to_all x0 -> x3, waiting for transfers between devices: none -> 58.7 us  [the longest x2 58.7 us: scatter_sum(): lax.all_to_all(part.reshape(S, walkers // S, nocc, m), 'stretch', 0, 0, t...]
    ppermute x0 -> x42, starting transfers between devices: none -> 57.7 us  [shift(): return lax.ppermute(a, 'stretch', pairs)]
  transfers between devices with their start and end apart: 5 -> 45, of which waited for: 4 -> 9; matrix products, arithmetic and copies ran while one was open for 17% -> 15% of each run, Pallas kernels for 0% -> 13%
where the time goes in v1:
time: 319 us; the launch traced here: 317 us
  Pallas kernels  84.5 us (26%)
  waiting for transfers between devices  76.7 us (24%)
  starting transfers between devices  74.4 us (23%)
  local copies, waits for them, and re-layouts  49.5 us (16%)
  blocking collectives  24.2 us (8%)
  other arithmetic  5.4 us (2%)
    all_to_all x2, waiting for transfers between devices, scatter_sum(): lax.all_to_all(part.reshape(S, walkers // S, nocc, m), 'stretch', 0, 0, t...  58.7 us
    ppermute x42, starting transfers between devices, shift(): return lax.ppermute(a, 'stretch', pairs)  57.7 us
    pallas_call x1, Pallas kernels, field_apply(): pl.pallas_call(field_kernel, grid=(m // 16,), in_specs=[pl.BlockSpec(memo...  43.7 us
    unnamed x63, local copies, waits for them, and re-layouts  25 us
    all_gather x1, blocking collectives, shards(): column = lax.all_gather(propagated, 'walk', axis=0, tiled=True)  24.2 us
    pallas_call x1, Pallas kernels, apply(): pl.pallas_call(apply_kernel, grid=(walkers // block,), in_specs=[pl.Block...  20.5 us
    pallas_call x1, Pallas kernels, intersect(): pl.pallas_call(intersect_kernel, grid=(steps,), in_specs=[pl.BlockSpec(me...  20.4 us
    ppermute x42, waiting for transfers between devices, shift(): return lax.ppermute(a, 'stretch', pairs)  17.9 us
  transfers between devices with their start and end apart: 45, of which 9 were waited for; matrix products, arithmetic and copies ran while one was open for 15% of the time, Pallas kernels for 13%

profile of v1, /device:TPU:1, one launch (start us, length us, event | category | flops | bytes accessed | tf_op | source)
XLA Modules:
  0.0 317.1 jit_solution(6146600774463860076)
XLA Ops:
  8.6 2.6 fusion.2
  14.2 2.5 copy.60
  18.1 4.1 %copy.61 = bf16[2048,512]{0,1:T(8,128)(2,1)} copy(bf16[2048,512]{1,0:T(8,128)(2,1)} %bitcast.27) | data formatting | bytes 4194304 | tf_op jit(solution)/shard_map/reshape | solution.py:127
  45.9 2.6 collective-permute-start.5
  55.1 3.7 %collective-permute-done.4 = bf16[8,48,512]{2,1,0:T(8,128)(2,1)S(1)} collective-permute-done((bf16[8,48,512]{2,1,0:T(8,128)(2,1)S(1)}, bf16[8,48,512]{2,1,0:T(8,128)(2,1)S(1)}, u32[]{:S(2)}, u32[]{:S(2)}) %collective-permute-start.4) | collective-permute-done | bytes 393248 | tf_op jit(solution)/shard_map/ppermute | solution.py:38
  58.8 2.7 collective-permute-start.13
  62.5 4.4 %collective-permute-start.19 = (bf16[8,48,512]{2,1,0:T(8,128)(2,1)}, bf16[8,48,512]{2,1,0:T(8,128)(2,1)}, u32[]{:S(2)}, u32[]{:S(2)}) collective-permute-start(bf16[8,48,512]{2,1,0:T(8,128)(2,1)} %get-tuple-element.50), channel_id=1, source_target_pairs={{0,24},{1,25},{2,26},{3,27},{4,28},{5,29},{6,30},{7,31},{8,0},{9,1... | collective-permute-start | bytes 1179656 | tf_op jit(solution)/shard_map/ppermute | solution.py:38
  67.3 2.7 collective-permute-done.13
  70.0 3.0 collective-permute-start.26
  74.2 20.4 %intersect.1 = (f32[32,2,8,128]{3,2,1,0:T(8,128)}, f32[32,2,16,128]{3,2,1,0:T(8,128)}) custom-call(s32[2,32]{1,0:T(2,128)} %dynamic-slice_bitcast_fusion.slot_ref, bf16[32,48,512]{2,1,0:T(8,128)(2,1)} %copy-done.12, bf16[32,48,512]{2,1,0:T(8,128)(2,1)} %copy-done.10, bf16[768,512]{1,0:T(8,128)(2,1)} %bitcast.32, bf16[768,512]{1,0:T(8,128)(2,1)} %bitcast.31, ...), custom_call_target="tpu_custom_call" | custom-call | flops 12884901888 | bytes 16777216 | tf_op jit(solution)/shard_map/intersect/pallas_call | solution.py:130
  106.6 43.7 %field_apply.1 = (bf16[64,512,512]{2,1,0:T(8,128)(2,1)}, bf16[64,48,512]{2,1,0:T(8,128)(2,1)}) custom-call(s32[2,32]{1,0:T(2,128)} %dynamic-slice_bitcast_fusion.slot_ref, bf16[64,32]{1,0:T(8,128)(2,1)} %multiply_convert_fusion.f_ref, bf16[32,48,512]{2,1,0:T(8,128)(2,1)} %constant_dynamic-update-slice_fusion.31.pa_ref, ...), custom_call_target="tpu_custom_call" | custom-call | flops 12884901888 | bytes 67108864 | tf_op jit(solution)/shard_map/field_apply/pallas_call | solution.py:209
  150.3 4.2 %all-to-all-start.1 = ((bf16[32,2,48,512]{3,2,1,0:T(8,128)(2,1)}), bf16[32,2,48,512]{3,2,1,0:T(8,128)(2,1)S(1)}, u32[]{:S(2)}, u32[]{:S(2)}) async-start(bf16[32,2,48,512]{3,2,1,0:T(8,128)(2,1)} %bitcast.28), calls=%async_computation.1 | async-start | bytes 6291456 | tf_op jit(solution)/shard_map/all_to_all | solution.py:265
  154.9 30.0 %all-to-all-done.1 = bf16[32,2,48,512]{3,2,1,0:T(8,128)(2,1)S(1)} async-done(((bf16[32,2,48,512]{3,2,1,0:T(8,128)(2,1)}), bf16[32,2,48,512]{3,2,1,0:T(8,128)(2,1)S(1)}, u32[]{:S(2)}, u32[]{:S(2)}) %all-to-all-start.1) | async-done | bytes 3145760 | tf_op jit(solution)/shard_map/all_to_all | solution.py:265
  187.8 2.9 collective-permute-done.28
  190.7 6.5 %collective-permute-start.29 = (bf16[2,48,512]{2,1,0:T(8,128)(2,1)S(1)}, bf16[2,48,512]{2,1,0:T(8,128)(2,1)S(1)}, u32[]{:S(2)}, u32[]{:S(2)}) collective-permute-start(bf16[2,48,512]{2,1,0:T(8,128)(2,1)S(1)} %pad_maximum_fusion.4), channel_id=1, source_target_pairs={{0,1},{1,2},{2,3},{3,0},{4,5},{5,6},{6,7},{7,4},{8,9},{9,10},{10,1... | collective-permute-start | bytes 294920 | tf_op jit(solution)/shard_map/ppermute | solution.py:38
  206.5 2.5 collective-permute-start.33
  212.1 7.1 %all-to-all-start = ((f32[32,1,2]{2,1,0:T(1,128)}), f32[32,1,2]{2,1,0:T(1,128)S(1)}, u32[]{:S(2)}, u32[]{:S(2)}) async-start(f32[32,1,2]{2,1,0:T(1,128)} %copy.67), calls=%async_computation | async-start | bytes 32768 | tf_op jit(solution)/shard_map/all_to_all | solution.py:283
  219.2 2.5 collective-permute-start.40
  226.8 4.3 %collective-permute-done.40 = bf16[8,48,512]{2,1,0:T(8,128)(2,1)S(1)} collective-permute-done((bf16[8,48,512]{2,1,0:T(8,128)(2,1)}, bf16[8,48,512]{2,1,0:T(8,128)(2,1)S(1)}, u32[]{:S(2)}, u32[]{:S(2)}) %collective-permute-start.40) | collective-permute-done | bytes 393248 | tf_op jit(solution)/shard_map/ppermute | solution.py:38
  231.1 3.0 collective-permute-done.41
  235.3 20.5 %apply.1 = bf16[64,48,512]{2,1,0:T(8,128)(2,1)} custom-call(s32[2,32]{1,0:T(2,128)} %dynamic-slice_bitcast_fusion.slot_ref, bf16[32,48,512]{2,1,0:T(8,128)(2,1)} %copy-done.4, bf16[32,48,512]{2,1,0:T(8,128)(2,1)} %copy-done.3, bf16[64,512,512]{2,1,0:T(8,128)(2,1)} %get-tuple-element.10.h_ref), custom_call_target="tpu_custom_call" | custom-call | flops 6442450944 | bytes 41943040 | tf_op jit(solution)/shard_map/apply/pallas_call | solution.py:246
  255.8 5.4 %all-to-all-start.2 = ((bf16[32,2,48,512]{3,2,1,0:T(8,128)(2,1)}), bf16[32,2,48,512]{3,2,1,0:T(8,128)(2,1)S(1)}, u32[]{:S(2)}, u32[]{:S(2)}) async-start(bf16[32,2,48,512]{3,2,1,0:T(8,128)(2,1)} %bitcast.26), calls=%async_computation.2 | async-start | bytes 6291456 | tf_op jit(solution)/shard_map/all_to_all | solution.py:265
  261.8 28.8 %all-to-all-done.2 = bf16[32,2,48,512]{3,2,1,0:T(8,128)(2,1)S(1)} async-done(((bf16[32,2,48,512]{3,2,1,0:T(8,128)(2,1)}), bf16[32,2,48,512]{3,2,1,0:T(8,128)(2,1)S(1)}, u32[]{:S(2)}, u32[]{:S(2)}) %all-to-all-start.2) | async-done | bytes 3145760 | tf_op jit(solution)/shard_map/all_to_all | solution.py:265
  291.5 24.2 %all_gather.3 = f32[8,48,512]{2,1,0:T(8,128)S(1)} all-gather(f32[2,48,512]{2,1,0:T(8,128)S(1)} %multiply_add_fusion), channel_id=1, replica_groups=mesh['walk'=4,'stretch'=32] {'walk'}, dimensions={0}, use_global_device_ids=true | all-gather | bytes 983040 | tf_op jit(solution)/shard_map/all_gather | solution.py:289
  (187 shorter events, 81.9 us)
Async XLA Ops:
  3.4 18.9 %collective-permute-start = (bf16[1,48,512]{2,1,0:T(8,128)(2,1)S(1)}, bf16[1,48,512]{2,1,0:T(8,128)(2,1)S(1)}, u32[]{:S(2)}, u32[]{:S(2)}) collective-permute-start(bf16[1,48,512]{2,1,0:T(8,128)(2,1)S(1)} %get-tuple-element.67), channel_id=1, source_target_pairs={{0,4},{1,5},{2,6},{3,7},{4,0},{5,1},{6,2},{7,3},{8,12},{9,13},{10,... | collective-permute-start | bytes 147464 | tf_op jit(solution)/shard_map/ppermute | solution.py:38
  5.5 19.6 %collective-permute-start.7 = (bf16[1,48,512]{2,1,0:T(8,128)(2,1)S(1)}, bf16[1,48,512]{2,1,0:T(8,128)(2,1)S(1)}, u32[]{:S(2)}, u32[]{:S(2)}) collective-permute-start(bf16[1,48,512]{2,1,0:T(8,128)(2,1)S(1)} %get-tuple-element.66), channel_id=1, source_target_pairs={{0,4},{1,5},{2,6},{3,7},{4,0},{5,1},{6,2},{7,3},{8,12},{9,13},{10,... | collective-permute-start | bytes 147464 | tf_op jit(solution)/shard_map/ppermute | solution.py:38
  7.1 19.6 %collective-permute-start.14 = (bf16[1,48,512]{2,1,0:T(8,128)(2,1)S(1)}, bf16[1,48,512]{2,1,0:T(8,128)(2,1)S(1)}, u32[]{:S(2)}, u32[]{:S(2)}) collective-permute-start(bf16[1,48,512]{2,1,0:T(8,128)(2,1)S(1)} %get-tuple-element.49), channel_id=1, source_target_pairs={{0,4},{1,5},{2,6},{3,7},{4,0},{5,1},{6,2},{7,3},{8,12},{9,13},{10,... | collective-permute-start | bytes 147464 | tf_op jit(solution)/shard_map/ppermute | solution.py:38
  8.6 19.9 %collective-permute-start.21 = (bf16[1,48,512]{2,1,0:T(8,128)(2,1)S(1)}, bf16[1,48,512]{2,1,0:T(8,128)(2,1)S(1)}, u32[]{:S(2)}, u32[]{:S(2)}) collective-permute-start(bf16[1,48,512]{2,1,0:T(8,128)(2,1)S(1)} %get-tuple-element.48), channel_id=1, source_target_pairs={{0,4},{1,5},{2,6},{3,7},{4,0},{5,1},{6,2},{7,3},{8,12},{9,13},{10,... | collective-permute-start | bytes 147464 | tf_op jit(solution)/shard_map/ppermute | solution.py:38
  26.7 12.4 %collective-permute-start.8 = (bf16[2,48,512]{2,1,0:T(8,128)(2,1)S(1)}, bf16[2,48,512]{2,1,0:T(8,128)(2,1)S(1)}, u32[]{:S(2)}, u32[]{:S(2)}) collective-permute-start(bf16[2,48,512]{2,1,0:T(8,128)(2,1)S(1)} %pad_maximum_fusion.1), channel_id=1, source_target_pairs={{0,8},{1,9},{2,10},{3,11},{4,12},{5,13},{6,14},{7,15},{8,16},{9,17... | collective-permute-start | bytes 294920 | tf_op jit(solution)/shard_map/ppermute | solution.py:38
  45.1 13.7 %collective-permute-start.4 = (bf16[8,48,512]{2,1,0:T(8,128)(2,1)S(1)}, bf16[8,48,512]{2,1,0:T(8,128)(2,1)S(1)}, u32[]{:S(2)}, u32[]{:S(2)}) collective-permute-start(bf16[8,48,512]{2,1,0:T(8,128)(2,1)S(1)} %get-tuple-element.68), channel_id=1, source_target_pairs={{0,8},{1,9},{2,10},{3,11},{4,12},{5,13},{6,14},{7,15},{8,16},{9,17... | collective-permute-start | bytes 1179656 | tf_op jit(solution)/shard_map/ppermute | solution.py:38
  45.9 15.6 %collective-permute-start.5 = (bf16[8,48,512]{2,1,0:T(8,128)(2,1)S(1)}, bf16[8,48,512]{2,1,0:T(8,128)(2,1)S(1)}, u32[]{:S(2)}, u32[]{:S(2)}) collective-permute-start(bf16[8,48,512]{2,1,0:T(8,128)(2,1)S(1)} %get-tuple-element.68), channel_id=1, source_target_pairs={{0,24},{1,25},{2,26},{3,27},{4,28},{5,29},{6,30},{7,31},{8,0},{9,1... | collective-permute-start | bytes 1179656 | tf_op jit(solution)/shard_map/ppermute | solution.py:38
  49.2 13.3 %collective-permute-start.6 = (bf16[8,48,512]{2,1,0:T(8,128)(2,1)S(1)}, bf16[8,48,512]{2,1,0:T(8,128)(2,1)S(1)}, u32[]{:S(2)}, u32[]{:S(2)}) collective-permute-start(bf16[8,48,512]{2,1,0:T(8,128)(2,1)S(1)} %get-tuple-element.68), channel_id=1, source_target_pairs={{0,16},{1,17},{2,18},{3,19},{4,20},{5,21},{6,22},{7,23},{8,24},{9,... | collective-permute-start | bytes 1179656 | tf_op jit(solution)/shard_map/ppermute | solution.py:38
  51.1 15.8 %collective-permute-start.11 = (bf16[8,48,512]{2,1,0:T(8,128)(2,1)}, bf16[8,48,512]{2,1,0:T(8,128)(2,1)S(1)}, u32[]{:S(2)}, u32[]{:S(2)}) collective-permute-start(bf16[8,48,512]{2,1,0:T(8,128)(2,1)} %get-tuple-element.56), channel_id=1, source_target_pairs={{0,1},{1,2},{2,3},{3,0},{4,5},{5,6},{6,7},{7,4},{8,9},{9,10},{10,1... | collective-permute-start | bytes 1179656 | tf_op jit(solution)/shard_map/ppermute | solution.py:38
  52.1 15.0 %collective-permute-start.12 = (bf16[8,48,512]{2,1,0:T(8,128)(2,1)}, bf16[8,48,512]{2,1,0:T(8,128)(2,1)S(1)}, u32[]{:S(2)}, u32[]{:S(2)}) collective-permute-start(bf16[8,48,512]{2,1,0:T(8,128)(2,1)} %get-tuple-element.56), channel_id=1, source_target_pairs={{0,3},{1,0},{2,1},{3,2},{4,7},{5,4},{6,5},{7,6},{8,11},{9,8},{10,9... | collective-permute-start | bytes 1179656 | tf_op jit(solution)/shard_map/ppermute | solution.py:38
  61.6 35.8 %collective-permute-start.18 = (bf16[8,48,512]{2,1,0:T(8,128)(2,1)}, bf16[8,48,512]{2,1,0:T(8,128)(2,1)S(1)}, u32[]{:S(2)}, u32[]{:S(2)}) collective-permute-start(bf16[8,48,512]{2,1,0:T(8,128)(2,1)} %get-tuple-element.50), channel_id=1, source_target_pairs={{0,8},{1,9},{2,10},{3,11},{4,12},{5,13},{6,14},{7,15},{8,16},{9,17... | collective-permute-start | bytes 1179656 | tf_op jit(solution)/shard_map/ppermute | solution.py:38
  62.5 36.9 %collective-permute-start.19 = (bf16[8,48,512]{2,1,0:T(8,128)(2,1)}, bf16[8,48,512]{2,1,0:T(8,128)(2,1)}, u32[]{:S(2)}, u32[]{:S(2)}) collective-permute-start(bf16[8,48,512]{2,1,0:T(8,128)(2,1)} %get-tuple-element.50), channel_id=1, source_target_pairs={{0,24},{1,25},{2,26},{3,27},{4,28},{5,29},{6,30},{7,31},{8,0},{9,1... | collective-permute-start | bytes 1179656 | tf_op jit(solution)/shard_map/ppermute | solution.py:38
  67.0 34.8 %collective-permute-start.20 = (bf16[8,48,512]{2,1,0:T(8,128)(2,1)}, bf16[8,48,512]{2,1,0:T(8,128)(2,1)S(1)}, u32[]{:S(2)}, u32[]{:S(2)}) collective-permute-start(bf16[8,48,512]{2,1,0:T(8,128)(2,1)} %get-tuple-element.50), channel_id=1, source_target_pairs={{0,16},{1,17},{2,18},{3,19},{4,20},{5,21},{6,22},{7,23},{8,24},{9,... | collective-permute-start | bytes 1179656 | tf_op jit(solution)/shard_map/ppermute | solution.py:38
  67.1 35.4 %collective-permute-start.25 = (bf16[8,48,512]{2,1,0:T(8,128)(2,1)}, bf16[8,48,512]{2,1,0:T(8,128)(2,1)S(1)}, u32[]{:S(2)}, u32[]{:S(2)}) collective-permute-start(bf16[8,48,512]{2,1,0:T(8,128)(2,1)} %copy-done.8), channel_id=1, source_target_pairs={{0,1},{1,2},{2,3},{3,0},{4,5},{5,6},{6,7},{7,4},{8,9},{9,10},{10,1... | collective-permute-start | bytes 1179656 | tf_op jit(solution)/shard_map/ppermute | solution.py:38
  70.0 34.0 %collective-permute-start.26 = (bf16[8,48,512]{2,1,0:T(8,128)(2,1)}, bf16[8,48,512]{2,1,0:T(8,128)(2,1)S(1)}, u32[]{:S(2)}, u32[]{:S(2)}) collective-permute-start(bf16[8,48,512]{2,1,0:T(8,128)(2,1)} %copy-done.8), channel_id=1, source_target_pairs={{0,3},{1,0},{2,1},{3,2},{4,7},{5,4},{6,5},{7,6},{8,11},{9,8},{10,9... | collective-permute-start | bytes 1179656 | tf_op jit(solution)/shard_map/ppermute | solution.py:38
  150.3 34.6 %all-to-all-start.1 = ((bf16[32,2,48,512]{3,2,1,0:T(8,128)(2,1)}), bf16[32,2,48,512]{3,2,1,0:T(8,128)(2,1)S(1)}, u32[]{:S(2)}, u32[]{:S(2)}) async-start(bf16[32,2,48,512]{3,2,1,0:T(8,128)(2,1)} %bitcast.28), calls=%async_computation.1 | async-start | bytes 6291456 | tf_op jit(solution)/shard_map/all_to_all | solution.py:265
  186.2 12.8 %collective-permute-start.35 = (bf16[1,48,512]{2,1,0:T(8,128)(2,1)S(1)}, bf16[1,48,512]{2,1,0:T(8,128)(2,1)S(1)}, u32[]{:S(2)}, u32[]{:S(2)}) collective-permute-start(bf16[1,48,512]{2,1,0:T(8,128)(2,1)S(1)} %get-tuple-element.30), channel_id=1, source_target_pairs={{0,4},{1,5},{2,6},{3,7},{4,0},{5,1},{6,2},{7,3},{8,12},{9,13},{10,... | collective-permute-start | bytes 147464 | tf_op jit(solution)/shard_map/ppermute | solution.py:38
  190.7 12.4 %collective-permute-start.29 = (bf16[2,48,512]{2,1,0:T(8,128)(2,1)S(1)}, bf16[2,48,512]{2,1,0:T(8,128)(2,1)S(1)}, u32[]{:S(2)}, u32[]{:S(2)}) collective-permute-start(bf16[2,48,512]{2,1,0:T(8,128)(2,1)S(1)} %pad_maximum_fusion.4), channel_id=1, source_target_pairs={{0,1},{1,2},{2,3},{3,0},{4,5},{5,6},{6,7},{7,4},{8,9},{9,10},{10,1... | collective-permute-start | bytes 294920 | tf_op jit(solution)/shard_map/ppermute | solution.py:38
  206.4 15.4 %collective-permute-start.32 = (bf16[8,48,512]{2,1,0:T(8,128)(2,1)}, bf16[8,48,512]{2,1,0:T(8,128)(2,1)}, u32[]{:S(2)}, u32[]{:S(2)}) collective-permute-start(bf16[8,48,512]{2,1,0:T(8,128)(2,1)} %get-tuple-element.32), channel_id=1, source_target_pairs={{0,8},{1,9},{2,10},{3,11},{4,12},{5,13},{6,14},{7,15},{8,16},{9,17... | collective-permute-start | bytes 1179656 | tf_op jit(solution)/shard_map/ppermute | solution.py:38
  206.5 16.8 %collective-permute-start.33 = (bf16[8,48,512]{2,1,0:T(8,128)(2,1)}, bf16[8,48,512]{2,1,0:T(8,128)(2,1)}, u32[]{:S(2)}, u32[]{:S(2)}) collective-permute-start(bf16[8,48,512]{2,1,0:T(8,128)(2,1)} %get-tuple-element.32), channel_id=1, source_target_pairs={{0,24},{1,25},{2,26},{3,27},{4,28},{5,29},{6,30},{7,31},{8,0},{9,1... | collective-permute-start | bytes 1179656 | tf_op jit(solution)/shard_map/ppermute | solution.py:38
  209.0 15.4 %collective-permute-start.34 = (bf16[8,48,512]{2,1,0:T(8,128)(2,1)}, bf16[8,48,512]{2,1,0:T(8,128)(2,1)}, u32[]{:S(2)}, u32[]{:S(2)}) collective-permute-start(bf16[8,48,512]{2,1,0:T(8,128)(2,1)} %get-tuple-element.32), channel_id=1, source_target_pairs={{0,16},{1,17},{2,18},{3,19},{4,20},{5,21},{6,22},{7,23},{8,24},{9,... | collective-permute-start | bytes 1179656 | tf_op jit(solution)/shard_map/ppermute | solution.py:38
  211.4 14.0 %collective-permute-start.39 = (bf16[8,48,512]{2,1,0:T(8,128)(2,1)}, bf16[8,48,512]{2,1,0:T(8,128)(2,1)}, u32[]{:S(2)}, u32[]{:S(2)}) collective-permute-start(bf16[8,48,512]{2,1,0:T(8,128)(2,1)} %get-tuple-element.20), channel_id=1, source_target_pairs={{0,1},{1,2},{2,3},{3,0},{4,5},{5,6},{6,7},{7,4},{8,9},{9,10},{10,1... | collective-permute-start | bytes 1179656 | tf_op jit(solution)/shard_map/ppermute | solution.py:38
  212.1 43.6 %all-to-all-start = ((f32[32,1,2]{2,1,0:T(1,128)}), f32[32,1,2]{2,1,0:T(1,128)S(1)}, u32[]{:S(2)}, u32[]{:S(2)}) async-start(f32[32,1,2]{2,1,0:T(1,128)} %copy.67), calls=%async_computation | async-start | bytes 32768 | tf_op jit(solution)/shard_map/all_to_all | solution.py:283
  255.8 34.8 %all-to-all-start.2 = ((bf16[32,2,48,512]{3,2,1,0:T(8,128)(2,1)}), bf16[32,2,48,512]{3,2,1,0:T(8,128)(2,1)S(1)}, u32[]{:S(2)}, u32[]{:S(2)}) async-start(bf16[32,2,48,512]{3,2,1,0:T(8,128)(2,1)} %bitcast.26), calls=%async_computation.2 | async-start | bytes 6291456 | tf_op jit(solution)/shard_map/all_to_all | solution.py:265
  (35 other events, 348.3 us)
